TPU v7x, 32 devices: a whole 2x2x4 slice. The times are simulated.
32 devices in a mesh: row: 8 (over z, x), col: 4 (over y, core).
Axes of the slice: x: 2, y: 2, z: 4, core: 2. Of those that a mesh axis runs over, the one named last changes fastest.
Arguments:
- coeffs: float32 [4096, 4096], P('row', 'col'), may hold values from -6 to 6
- ham_alpha: float32 [4096, 4096], P('row'), may hold values from -1.5 to 7.5, as said below
- ham_beta: float32 [4096, 4096], P('col'), may hold values from -1.5 to 7.5, as said below
Outputs:
- sigma_vec: float32 [4096, 4096], P('row', 'col')
Inputs may be any that keep to these rules, and one draw needn't show every extreme that they name: `ham_alpha`: symmetric. `ham_beta`: symmetric.
All inputs are finite; a program needn't handle non-finite values.
Results may differ from a plain program's by a relative error of at most 0.00005.
Values sent between devices are 32-bit elements; how exact they have to be, the bound alone decides.
A program may use at most 128 MiB of HBM per device.

v0:
```python
import jax
import jax.numpy as jnp
from jax import lax
from jax.sharding import PartitionSpec as P

HIGHEST = lax.Precision.HIGHEST


def local(coeffs, ham_alpha, ham_beta):
    ham_cols = ham_alpha
    alpha_part = jnp.dot(
        ham_cols,
        lax.all_gather(coeffs, "row", axis=0, tiled=True),
        precision=HIGHEST,
        preferred_element_type=jnp.float32,
    )
    ham_cols = ham_beta
    flipped = lax.psum_scatter(
        lax.dot_general(
            ham_cols,
            coeffs,
            (((0,), (1,)), ((), ())),
            precision=HIGHEST,
            preferred_element_type=jnp.float32,
        ),
        "col",
        scatter_dimension=0,
        tiled=True,
    )
    beta_part = flipped.T
    return alpha_part + beta_part


def solution(mesh):
    in_specs = (P("row", "col"), P("row", None), P("col", None))
    out_specs = P("row", "col")
    return jax.shard_map(local, mesh=mesh, in_specs=in_specs, out_specs=out_specs, check_vma=False)
```

profile of v0, /device:TPU:0, one launch (start us, length us, event | category | flops | bytes accessed | tf_op | source)
XLA Modules:
  0.0 311.4 jit_solution(360071280778495948)
XLA Ops:
  7.4 0.0 reduce-scatter.2.cloned.1.call-start
  7.4 31.3 %fusion = f32[4096,512]{0,1:T(8,128)} fusion(f32[1024,4096]{1,0:T(8,128)} %param.5, f32[512,1024]{1,0:T(8,128)} %param.3), kind=kOutput, calls=%fused_computation.1 | convolution fusion | flops 25769803776 | bytes 27262976 | tf_op jit(solution)/shard_map/dot_general | solution.py:19
  38.7 0.0 reduce-scatter.2.cloned.1.call-update
  38.7 0.2 all-gather.2.cloned.1.call-start
  39.0 0.3 all-gather.2.cloned.1.call-update
  39.3 73.5 %reduce-scatter.2.cloned.1.call-done = f32[1024,512]{0,1:T(8,128)} async-done(((f32[4096,512]{0,1:T(8,128)}), f32[1024,512]{0,1:T(8,128)}) %reduce-scatter.2.cloned.1.call-update) | async-done | bytes 2097168 | tf_op jit(solution)/shard_map/reduce_scatter | solution.py:18
  112.8 158.3 %all-gather.2.cloned.1.call-done = f32[4096,1024]{1,0:T(8,128)} async-done(((f32[512,1024]{1,0:T(8,128)}), f32[4096,1024]{1,0:T(8,128)}) %all-gather.2.cloned.1.call-update) | async-done | bytes 16777232 | tf_op jit(solution)/shard_map/all_gather | solution.py:13
  271.2 32.7 %bitcast_add_fusion = f32[512,1024]{1,0:T(8,128)} fusion(f32[1024,512]{0,1:T(8,128)} %reduce-scatter.2.cloned.1.call-done, f32[512,4096]{1,0:T(8,128)} %param.4, f32[4096,1024]{1,0:T(8,128)} %all-gather.2.cloned.1.call-done), kind=kOutput, calls=%fused_computation | convolution fusion | flops 25770328064 | bytes 29360128 | tf_op jit(solution)/shard_map/dot_general | solution.py:11
Async XLA Ops:
  7.4 105.5 %reduce-scatter.2.cloned.1.call-start = ((), (), s32[]{:S(2)}) async-start(), calls=%async_computation.2 | async-start | bytes 10485760 | tf_op jit(solution)/shard_map/reduce_scatter | solution.py:18
  38.7 232.5 %all-gather.2.cloned.1.call-start = ((), (), s32[]{:S(2)}) async-start(), calls=%async_computation.1 | async-start | bytes 18874368 | tf_op jit(solution)/shard_map/all_gather | solution.py:13
Sparse Core Ops, SparseCore 0:
  38.8 73.9 reduce-scatter.1
Sparse Core Ops, SparseCore 1:
  41.3 229.8 all-gather.1
where the time goes:
time: 312 us; the launch traced here: 311 us
  waiting for transfers between devices  232 us (74%)
  matrix products  64.1 us (21%)
  between operations  14.8 us (5%)
    all_gather x1, waiting for transfers between devices, local(): lax.all_gather(coeffs, 'row', axis=0, tiled=True)  158 us
    reduce_scatter x1, waiting for transfers between devices, local(): lax.psum_scatter(lax.dot_general(ham_cols, coeffs, (((0,), (1,)), ((), ()...  73.5 us
    dot_general x1, matrix products, local(): jnp.dot(ham_cols, lax.all_gather(coeffs, 'row', axis=0, tiled=True), prec...  32.7 us
    dot_general x1, matrix products, local(): lax.dot_general(ham_cols, coeffs, (((0,), (1,)), ((), ())), precision=HIG...  31.3 us
  transfers between devices with their start and end apart: 2, of which 2 were waited for; matrix products, arithmetic and copies ran while one was open for 0% of the time, Pallas kernels for 0%

commit v1 on v0

v1 whole, which is shorter than its diff:
```python
import functools

import jax
import jax.numpy as jnp
from jax import lax
from jax.experimental import pallas as pl
from jax.experimental.pallas import tpu as pltpu
from jax.sharding import PartitionSpec as P

PAIR = 2
MESH = pl.DeviceIdType.MESH


def flip(index, key):
    bit = 1
    while bit <= key:
        if key & bit:
            index = index + bit - 2 * bit * ((index // bit) % 2)
        bit *= 2
    return index


def split(value):
    high = value.astype(jnp.bfloat16)
    return high, (value - high.astype(jnp.float32)).astype(jnp.bfloat16)


def product(lhs, rhs, rhs_dim):
    lhs_high, lhs_low = split(lhs)
    rhs_high, rhs_low = split(rhs)

    def one(a, b):
        return lax.dot_general(
            a, b, (((1,), (rhs_dim,)), ((), ())), preferred_element_type=jnp.float32
        )

    return one(lhs_high, rhs_high) + (one(lhs_high, rhs_low) + one(lhs_low, rhs_high))


def exchanges(n):
    held, mask, out = [0], n // 2, []
    while mask:
        out += [(mask, key) for key in held]
        held += [key ^ mask for key in held]
        mask //= 2
    return out


def kernel(
    line, cols_n, cw, width,
    coeffs, ha, hb, out,
    ham, beta, co, ag, sums, sums_in, acc, acc_in, turned, back_in,
    load_sem, ag_send, ag_recv, s_send, s_recv, o_send, o_recv,
    x_send, x_recv, p_send, p_recv, c_send, c_recv,
):
    rows, cols = coeffs.shape
    nk = cols // cw - 1
    row, col = lax.axis_index("row"), lax.axis_index("col")
    z, x = row // PAIR, row % PAIR
    partner = z * PAIR + 1 - x
    steps = exchanges(cols_n)
    masks = sorted({mask for mask, _ in steps}, reverse=True)

    def there(to_row, to_col):
        return (to_row, to_col)

    def ham_load(s):
        at = pl.multiple_of((s * PAIR + x) * rows, 128)
        return pltpu.make_async_copy(ha.at[:, pl.ds(at, rows)], ham.at[0, s], load_sem.at[s])

    def beta_load(key):
        at = pl.multiple_of(flip(col, key) * cols, 128)
        return pltpu.make_async_copy(
            hb.at[:, pl.ds(at, cols)], beta.at[key], load_sem.at[line + key]
        )

    beta_load(0).start()
    for s in range(line):
        ham_load(s).start()
    for key in range(1, cols_n):
        beta_load(key).start()

    barrier = pltpu.get_barrier_semaphore()
    has_low, has_high = z > 0, z < line - 1
    pl.semaphore_signal(barrier, inc=1, device_id=there(partner, col), device_id_type=MESH)
    for mask in masks:
        pl.semaphore_signal(
            barrier, inc=1, device_id=there(row, flip(col, mask)), device_id_type=MESH
        )

    @pl.when(has_low)
    def _():
        pl.semaphore_signal(barrier, inc=1, device_id=there(row - PAIR, col), device_id_type=MESH)

    @pl.when(has_high)
    def _():
        pl.semaphore_signal(barrier, inc=1, device_id=there(row + PAIR, col), device_id_type=MESH)

    inner = jnp.logical_and(has_low, has_high)

    @pl.when(inner)
    def _():
        pl.semaphore_wait(barrier, 3 + len(masks))

    @pl.when(jnp.logical_not(inner))
    def _():
        pl.semaphore_wait(barrier, 2 + len(masks))

    def remote(src, dst, send, recv, to):
        return pltpu.make_async_remote_copy(
            src_ref=src, dst_ref=dst, send_sem=send, recv_sem=recv,
            device_id=to, device_id_type=MESH,
        )

    def slot(index):
        first = index * width
        at = pl.multiple_of(first % rows, 128)
        return ham.at[1, first // rows, :, pl.ds(at, width)]

    def piece_copy():
        first = col * width
        at = pl.multiple_of((first // rows * PAIR + 1 - x) * rows + first % rows, 128)
        return remote(
            ha.at[:, pl.ds(at, width)], slot(col), x_send.at[0], x_recv.at[0], there(partner, col)
        )

    def back_copy():
        return remote(
            coeffs.at[:, pl.ds(nk * cw, cw)], back_in, x_send.at[1], x_recv.at[1],
            there(partner, col),
        )

    def other_copy(k):
        return remote(acc.at[1, k], acc_in.at[k], o_send.at[k], o_recv.at[k], there(partner, col))

    def ag_copy(d, t, k):
        src = coeffs.at[:, pl.ds(pl.multiple_of(k * cw, 128), cw)] if t == 1 else ag.at[d, t - 2, k]
        to = there(row + PAIR if d == 0 else row - PAIR, col)
        return remote(src, ag.at[d, t - 1, k], ag_send.at[d, t - 1, k], ag_recv.at[d, t - 1, k], to)

    def ag_sends(d, t):
        if d == 0:
            return jnp.logical_and(has_high, z >= t - 1)
        return jnp.logical_and(has_low, z <= line - t)

    def ag_gets(d, t):
        return z >= t if d == 0 else z <= line - 1 - t

    def s_copy(d, m):
        to = there(row + PAIR if d == 0 else row - PAIR, col)
        return remote(sums.at[d, m - 1], sums_in.at[d, m - 1], s_send.at[d, m - 1], s_recv.at[d, m - 1], to)

    def s_sends(d, m):
        return z <= line - 1 - m if d == 0 else z >= m

    def s_gets(d, m):
        if d == 0:
            return jnp.logical_and(z >= 1, z - 1 <= line - 1 - m)
        return jnp.logical_and(z <= line - 2, z + 1 >= m)

    def p_copy(i):
        mask, key = steps[i]
        place = slot(flip(col, key))
        return remote(place, place, p_send.at[i], p_recv.at[i], there(row, flip(col, mask)))

    def p_got(i):
        mask, key = steps[i]
        place = slot(flip(col, key ^ mask))
        return remote(place, place, p_send.at[i], p_recv.at[i], there(row, flip(col, mask)))

    half = rows // 2

    def c_copy(i, h):
        mask, key = steps[i]
        part = pl.ds(h * half, half)
        src = coeffs.at[part] if key == 0 else co.at[key - 1, part]
        return remote(
            src, co.at[(key ^ mask) - 1, part], c_send.at[i, h], c_recv.at[i, h],
            there(row, flip(col, mask)),
        )

    piece_copy().start()
    for d in range(2):
        @pl.when(ag_sends(d, 1))
        def _(d=d):
            for k in range(nk):
                ag_copy(d, 1, k).start()
    c_copy(0, 0).start()
    back_copy().start()

    tile = min(256, cols)

    def beta_tile(key_ref, beta_ref, n, add):
        at = pl.ds(pl.multiple_of(n * tile, 128), tile)
        value = product(key_ref[...], beta_ref[at, :], 1)
        out[:, at] = out[:, at] + value if add else value

    beta_load(0).wait()

    @pl.loop(0, cols // tile)
    def _(n):
        beta_tile(coeffs, beta.at[0], n, False)

    turned[0] = coeffs[:, nk * cw:].T
    for s in range(line):
        ham_load(s).wait()
    for key in range(1, cols_n):
        beta_load(key).wait()

    piece_copy().wait_recv()
    p_copy(0).start()
    c_copy(0, 1).start()

    def pass_on(t):
        for k in range(nk):
            for d in range(2):
                @pl.when(ag_gets(d, t))
                def _(d=d, k=k):
                    ag_copy(d, t, k).wait_recv()

                if t + 1 < line:
                    @pl.when(ag_sends(d, t + 1))
                    def _(d=d, k=k):
                        ag_copy(d, t + 1, k).start()

    pass_on(1)

    for mask in masks:
        group = [i for i, step in enumerate(steps) if step[0] == mask]
        for i in group:
            if i:
                p_copy(i).start()
        for i in group:
            p_got(i).wait_recv()
    back_copy().wait_recv()
    turned[1] = back_in[...].T

    def term(s):
        def body(m, total):
            return total + product(turned[m], ham[m, s], 0)

        return lax.fori_loop(0, PAIR, body, jnp.zeros((cw, rows), jnp.float32))

    def send_sums(m):
        for d in range(2):
            @pl.when(s_sends(d, m))
            def _(d=d):
                sums[d, m - 1] = term(z + m if d == 0 else z - m)

            if m + 1 < line:
                @pl.when(s_gets(d, m + 1))
                def _(d=d):
                    s_copy(d, m + 1).wait_recv()

                @pl.when(jnp.logical_and(s_gets(d, m + 1), s_sends(d, m)))
                def _(d=d):
                    sums[d, m - 1] = sums[d, m - 1] + sums_in[d, m]

            @pl.when(s_sends(d, m))
            def _(d=d):
                s_copy(d, m).start()

    def add_products(d, t, k):
        s = z - t if d == 0 else z + t

        @pl.loop(0, PAIR)
        def _(m):
            acc[m, k] = acc[m, k] + product(ham[m, s], ag[d, t - 1, k], 0)

    def add_step(t):
        for d in range(2):
            @pl.when(ag_gets(d, t))
            def _(d=d):
                @pl.loop(0, nk)
                def _(k):
                    add_products(d, t, k)

    if line > 1:
        send_sums(line - 1)

    @pl.loop(0, nk)
    def _(k):
        own = coeffs.at[:, pl.ds(pl.multiple_of(k * cw, 128), cw)]

        @pl.loop(0, PAIR)
        def _(m):
            acc[m, k] = product(ham[m, z], own[...], 0)

    def coeffs_step(mask):
        group = [i for i, step in enumerate(steps) if step[0] == mask]
        for i in group:
            if i:
                for h in range(2):
                    c_copy(i, h).start()
        for i in group:
            for h in range(2):
                c_copy(i, h).wait_recv()

    add_step(1)
    for t in range(2, line):
        if t < line - 1:
            pass_on(t)
        send_sums(line - t)
        if t == 2:
            coeffs_step(masks[0])
            if len(masks) > 1:
                for i, step in enumerate(steps):
                    if step[0] == masks[1]:
                        for h in range(2):
                            c_copy(i, h).start()
        if t < line - 1:
            add_step(t)

    for j, mask in enumerate(masks):
        group = [i for i, step in enumerate(steps) if step[0] == mask]
        if j >= 2:
            for i in group:
                for h in range(2):
                    c_copy(i, h).start()
        if j >= 1:
            for i in group:
                for h in range(2):
                    c_copy(i, h).wait_recv()

    @pl.loop(1, cols_n)
    def _(key):
        @pl.loop(0, cols // tile)
        def _(n):
            beta_tile(co.at[key - 1], beta.at[key], n, True)

    t = line - 1

    @pl.loop(0, nk)
    def _(k):
        for d in range(2):
            @pl.when(ag_gets(d, t))
            def _(d=d):
                ag_copy(d, t, k).wait_recv()
                add_products(d, t, k)

        other_copy(k).start()

    tail = term(z)
    for d in range(2):
        @pl.when(s_gets(d, 1))
        def _(d=d):
            s_copy(d, 1).wait_recv()
    sums[0, line - 1] = tail
    for d in range(2):
        @pl.when(s_gets(d, 1))
        def _(d=d):
            sums[0, line - 1] = sums[0, line - 1] + sums_in[d, 0]
    out[:, nk * cw:] = out[:, nk * cw:] + sums[0, line - 1].T

    @pl.loop(0, nk)
    def _(k):
        at = pl.ds(pl.multiple_of(k * cw, 128), cw)
        other_copy(k).wait_recv()
        out[:, at] = out[:, at] + (acc[0, k] + acc_in[k])

    piece_copy().wait_send()
    back_copy().wait_send()
    for i in range(len(steps)):
        p_copy(i).wait_send()
        for h in range(2):
            c_copy(i, h).wait_send()
    for d in range(2):
        for m in range(1, line):
            @pl.when(ag_sends(d, m))
            def _(d=d, m=m):
                for k in range(nk):
                    ag_copy(d, m, k).wait_send()

            @pl.when(s_sends(d, m))
            def _(d=d, m=m):
                s_copy(d, m).wait_send()

    @pl.loop(0, nk)
    def _(k):
        other_copy(k).wait_send()


def solution(mesh):
    line, cols_n = mesh.shape["row"] // PAIR, mesh.shape["col"]
    n_steps = len(exchanges(cols_n))

    def local(coeffs, ham_alpha, ham_beta):
        rows, cols = coeffs.shape
        cw = min(256, cols // 2)
        nk = cols // cw - 1
        width = line * rows // cols_n
        f32, dma = jnp.float32, pltpu.SemaphoreType.DMA
        any_spec = pl.BlockSpec(memory_space=pl.ANY)
        vmem_spec = pl.BlockSpec(memory_space=pltpu.VMEM)
        return pl.pallas_call(
            functools.partial(kernel, line, cols_n, cw, width),
            out_shape=jax.ShapeDtypeStruct((rows, cols), f32),
            in_specs=[vmem_spec, any_spec, any_spec],
            out_specs=vmem_spec,
            scratch_shapes=[
                pltpu.VMEM((PAIR, line, rows, rows), f32),
                pltpu.VMEM((cols_n, cols, cols), f32),
                pltpu.VMEM((cols_n - 1, rows, cols), f32),
                pltpu.VMEM((2, line - 1, nk, rows, cw), f32),
                pltpu.VMEM((2, line, cw, rows), f32),
                pltpu.VMEM((2, line - 1, cw, rows), f32),
                pltpu.VMEM((PAIR, nk, rows, cw), f32),
                pltpu.VMEM((nk, rows, cw), f32),
                pltpu.VMEM((PAIR, cw, rows), f32),
                pltpu.VMEM((rows, cw), f32),
                dma((line + cols_n,)),
                dma((2, line - 1, nk)),
                dma((2, line - 1, nk)),
                dma((2, line - 1)),
                dma((2, line - 1)),
                dma((nk,)),
                dma((nk,)),
                dma((2,)),
                dma((2,)),
                dma((n_steps,)),
                dma((n_steps,)),
                dma((n_steps, 2)),
                dma((n_steps, 2)),
            ],
            compiler_params=pltpu.CompilerParams(
                collective_id=0, has_side_effects=True, vmem_limit_bytes=67043328
            ),
        )(coeffs, ham_alpha, ham_beta)

    in_specs = (P("row", "col"), P("row", None), P("col", None))
    return jax.shard_map(
        local, mesh=mesh, in_specs=in_specs, out_specs=P("row", "col"), check_vma=False
    )
```

time: 312 us -> 139 us (0.45)
  the two profiles are of different devices: /device:TPU:0 before, /device:TPU:16 now
where the time goes in v1:
time: 139 us
  Pallas kernels  136 us (98%)
  local copies, waits for them, and re-layouts  3.16 us (2%)
    pallas_call x1, Pallas kernels, local(): pl.pallas_call(functools.partial(kernel, line, cols_n, cw, width), out_sh...  136 us
    unnamed x1, local copies, waits for them, and re-layouts  3.16 us

profile of v1, /device:TPU:16, one launch (start us, length us, event | category | flops | bytes accessed | tf_op | source)
XLA Modules:
  0.0 139.2 jit_solution(3328450595973626309)
XLA Ops:
  0.0 136.0 %shard_map.37 = f32[512,1024]{1,0:T(8,128)} custom-call(f32[512,1024]{1,0:T(8,128)} %coeffs.1, f32[512,4096]{1,0:T(8,128)} %ha.1, f32[1024,4096]{1,0:T(8,128)} %hb.1), custom_call_target="tpu_custom_call" | custom-call | tf_op jit(solution)/shard_map/pallas_call | solution.py:395
  136.0 3.2 %copy.5 = f32[512,1024]{1,0:T(8,128)} copy(f32[512,1024]{1,0:T(8,128)} %shard_map.37) | data formatting | bytes 4194304

commit v2 on v1

--- a/solution.py
+++ b/solution.py
@@ -211,8 +211,8 @@
     p_copy(0).start()
     c_copy(0, 1).start()
 
-    def pass_on(t):
-        for k in range(nk):
+    def pass_on(t, ks):
+        for k in ks:
             for d in range(2):
                 @pl.when(ag_gets(d, t))
                 def _(d=d, k=k):
@@ -223,7 +223,7 @@
                     def _(d=d, k=k):
                         ag_copy(d, t + 1, k).start()
 
-    pass_on(1)
+    pass_on(1, range(nk))
 
     for mask in masks:
         group = [i for i, step in enumerate(steps) if step[0] == mask]
@@ -275,8 +275,12 @@
                 def _(k):
                     add_products(d, t, k)
 
-    if line > 1:
-        send_sums(line - 1)
+    early = line > 3
+    if early:
+        pass_on(2, range(min(1, nk)))
+    send_sums(line - 1)
+    if early:
+        pass_on(2, range(1, nk - 1))
 
     @pl.loop(0, nk)
     def _(k):
@@ -296,11 +300,13 @@
             for h in range(2):
                 c_copy(i, h).wait_recv()
 
-    add_step(1)
+    if early:
+        pass_on(2, range(max(1, nk - 1), nk))
     for t in range(2, line):
+        if 2 < t < line - 1:
+            pass_on(t, range(nk))
         if t < line - 1:
-            pass_on(t)
-        send_sums(line - t)
+            send_sums(line - t)
         if t == 2:
             coeffs_step(masks[0])
             if len(masks) > 1:
@@ -308,37 +314,43 @@
                     if step[0] == masks[1]:
                         for h in range(2):
                             c_copy(i, h).start()
-        if t < line - 1:
-            add_step(t)
-
-    for j, mask in enumerate(masks):
-        group = [i for i, step in enumerate(steps) if step[0] == mask]
-        if j >= 2:
-            for i in group:
-                for h in range(2):
-                    c_copy(i, h).start()
-        if j >= 1:
-            for i in group:
-                for h in range(2):
-                    c_copy(i, h).wait_recv()
-
-    @pl.loop(1, cols_n)
-    def _(key):
+        add_step(t - 1)
+
+    def coeffs_rest():
+        for j, mask in enumerate(masks):
+            group = [i for i, step in enumerate(steps) if step[0] == mask]
+            if j >= 2:
+                for i in group:
+                    for h in range(2):
+                        c_copy(i, h).start()
+            if j >= 1:
+                for i in group:
+                    for h in range(2):
+                        c_copy(i, h).wait_recv()
+
+    def add_beta(key):
         @pl.loop(0, cols // tile)
         def _(n):
             beta_tile(co.at[key - 1], beta.at[key], n, True)
 
     t = line - 1
-
-    @pl.loop(0, nk)
-    def _(k):
+    for k in range(nk):
         for d in range(2):
             @pl.when(ag_gets(d, t))
-            def _(d=d):
+            def _(d=d, k=k):
                 ag_copy(d, t, k).wait_recv()
                 add_products(d, t, k)
 
         other_copy(k).start()
+        if k == 0:
+            send_sums(1)
+            coeffs_rest()
+        if k + 1 < cols_n:
+            add_beta(k + 1)
+
+    @pl.loop(nk + 1, cols_n)
+    def _(key):
+        add_beta(key)
 
     tail = term(z)
     for d in range(2):

time: 139 us -> 127 us (0.914)
  the two profiles are of different devices: /device:TPU:16 before, /device:TPU:0 now
where the time goes in v2:
time: 127 us
  Pallas kernels  124 us (98%)
  local copies, waits for them, and re-layouts  3.16 us (2%)
    pallas_call x1, Pallas kernels, local(): pl.pallas_call(functools.partial(kernel, line, cols_n, cw, width), out_sh...  124 us
    unnamed x1, local copies, waits for them, and re-layouts  3.16 us

profile of v2, /device:TPU:0, one launch (start us, length us, event | category | flops | bytes accessed | tf_op | source)
XLA Modules:
  0.0 126.9 jit_solution(8796416019306074143)
XLA Ops:
  0.0 123.7 %shard_map.37 = f32[512,1024]{1,0:T(8,128)} custom-call(f32[512,1024]{1,0:T(8,128)} %coeffs.1, f32[512,4096]{1,0:T(8,128)} %ha.1, f32[1024,4096]{1,0:T(8,128)} %hb.1), custom_call_target="tpu_custom_call" | custom-call | tf_op jit(solution)/shard_map/pallas_call | solution.py:407
  123.7 3.2 %copy.5 = f32[512,1024]{1,0:T(8,128)} copy(f32[512,1024]{1,0:T(8,128)} %shard_map.37) | data formatting | bytes 4194304
